TPU v7x, 512 devices: a whole 4x4x16 slice. The times are simulated.
512 devices in a mesh: ctx: 64 (over x, z), fsdp: 8 (over y, core).
Axes of the slice: x: 4, y: 4, z: 16, core: 2. Of those that a mesh axis runs over, the one named last changes fastest.
Arguments:
- tokens: bfloat16 [8, 8192, 4096], P('fsdp', 'ctx'), may hold values from -6 to 6
- queries: bfloat16 [8, 8192, 512], P('fsdp', 'ctx'), may hold values from -6 to 6
- flags: int32 [8, 8192], P('fsdp', 'ctx'), may hold values from 0 to 1, as said below
- w_key: bfloat16 [4096, 512], P(('ctx', 'fsdp')), may hold values from -0.09375 to 0.09375
- w_value: bfloat16 [4096, 512], P(('ctx', 'fsdp')), may hold values from -0.09375 to 0.09375
- norm_gain: float32 [512], replicated, may hold values from 0.25 to 1.75
Outputs:
- attended: bfloat16 [8, 8192, 512], P('fsdp', 'ctx')
Inputs may be any that keep to these rules, and one draw needn't show every extreme that they name: `flags`: in each sequence a document starts at token 0 and at every token k * 2048 + 2048 // 2; other tokens start one at random, never before token 3072 and never at the first token of a block. No document is longer than 2048 tokens.
All inputs are finite; a program needn't handle non-finite values.
Results may differ from a plain program's by a relative error of at most 0.0053.
Values may be sent and summed in bfloat16 or wider, within the bound.
A program may use at most 64 MiB of HBM per device.

v0:
```python
import jax
import jax.numpy as jnp
from jax import lax
from jax.sharding import PartitionSpec as P

HEAD = 128


def entering(array, axis, join, neutral):
    place = lax.axis_index(axis)
    gathered = jax.tree.map(
        lambda a, kind: lax.all_gather(a.astype(kind), axis), array, (jnp.bfloat16, jnp.bfloat16)
    )
    state = jax.tree.map(lambda a, e: jnp.zeros_like(a) + jnp.asarray(e, a.dtype), array, neutral)

    def one(lap, state):
        return join(
            state,
            jax.tree.map(
                lambda a, own: lax.dynamic_index_in_dim(a, lap, 0, False).astype(own.dtype),
                gathered,
                array,
            ),
        )

    return lax.fori_loop(0, place, one, state)


def feature(u):
    return jax.nn.elu(u) + 1.0


def combine(earlier, later):
    keep = 1.0 - later[0][0]
    return (jnp.maximum(earlier[0], later[0]), later[1] + keep * earlier[1])


def on_device(tokens, queries, flags, w_key, w_value, norm_gain):
    rows = tokens[0]
    count = rows.shape[0]
    width = w_key.shape[1]
    heads = width // HEAD
    full_panels = (
        lax.all_gather(w_key, ("ctx", "fsdp"), axis=0, tiled=True),
        lax.all_gather(w_value, ("ctx", "fsdp"), axis=0, tiled=True),
    )
    proj_key = jnp.dot(rows, full_panels[0], preferred_element_type=jnp.float32)
    proj_value = jnp.dot(rows, full_panels[1], preferred_element_type=jnp.float32)
    key = feature(proj_key).astype(jnp.bfloat16).reshape(count, heads, HEAD)
    value = proj_value.astype(jnp.bfloat16).reshape(count, heads, HEAD)
    query = feature(queries[0].astype(jnp.float32)).astype(jnp.bfloat16).reshape(count, heads, HEAD)
    seg = jnp.cumsum(flags[0])
    last = seg[count - 1]
    reset = (last > 0).astype(jnp.float32).reshape(1)
    tail = (seg == last).astype(jnp.bfloat16)
    local_state = jnp.einsum(
        "the,thf->hef", key * tail[:, None, None], value, preferred_element_type=jnp.float32
    )
    identity = (jnp.zeros((1,), jnp.float32), jnp.zeros_like(local_state))
    carried = entering((reset, local_state), "ctx", combine, identity)
    carried_b = carried[1].astype(jnp.bfloat16)
    places = jnp.arange(count, dtype=jnp.int32)
    allowed = (places[None, :] <= places[:, None]) & (seg[None, :] == seg[:, None])
    scores = jnp.einsum("the,she->hts", query, key, preferred_element_type=jnp.float32)
    scores = jnp.where(allowed[None, :, :], scores, 0.0).astype(jnp.bfloat16)
    inside = jnp.einsum("hts,shf->thf", scores, value, preferred_element_type=jnp.float32)
    first = (seg == 0).astype(jnp.float32)
    carried_term = (
        jnp.einsum("the,hef->thf", query, carried_b, preferred_element_type=jnp.float32)
        * first[:, None, None]
    )
    mixed = carried_term + inside
    scale = lax.rsqrt(jnp.mean(mixed * mixed, axis=-1, keepdims=True) + 1e-06)
    attended = (mixed * scale * norm_gain.reshape(heads, HEAD)).astype(jnp.bfloat16)
    return attended.reshape(1, count, width)


def solution(mesh):
    in_specs = (
        P("fsdp", "ctx", None),
        P("fsdp", "ctx", None),
        P("fsdp", "ctx"),
        P(("ctx", "fsdp"), None),
        P(("ctx", "fsdp"), None),
        P(),
    )
    out_specs = P("fsdp", "ctx", None)
    return jax.shard_map(
        on_device, mesh=mesh, in_specs=in_specs, out_specs=out_specs, check_vma=False
    )
```

profile of v0, /device:TPU:486, one launch (start us, length us, event | category | flops | bytes accessed | tf_op | source)
XLA Modules:
  0.0 710.5 jit_solution(16022774016434404635)
XLA Ops:
  10.1 196.2 %all-gather.7.cloned.1.call-done = bf16[4096,512]{1,0:T(8,128)(2,1)} async-done(((bf16[8,512]{1,0:T(8,128)(2,1)}), bf16[4096,512]{1,0:T(8,128)(2,1)}) %all-gather.7.cloned.1.call-update) | async-done | bytes 4194320 | tf_op jit(solution)/shard_map/all_gather | solution.py:45
  206.4 2.9 convolution_convert_fusion
  209.4 195.0 %all-gather.5.cloned.1.call-done = bf16[4096,512]{1,0:T(8,128)(2,1)} async-done(((bf16[8,512]{1,0:T(8,128)(2,1)}), bf16[4096,512]{1,0:T(8,128)(2,1)}) %all-gather.5.cloned.1.call-update) | async-done | bytes 4194320 | tf_op jit(solution)/shard_map/all_gather | solution.py:44
  404.4 3.0 fusion.11
  411.1 138.5 %all-reduce = bf16[64]{0:T(256)(128)(2,1)S(1)} all-reduce(bf16[64]{0:T(256)(128)(2,1)S(1)} %dynamic-update-slice), channel_id=1, replica_groups=mesh['ctx'=64,'fsdp'=8] {'ctx'}, use_global_device_ids=true, to_apply=%add | all-reduce | flops 64 | bytes 256
  549.6 10.8 %all-gather.9.cloned.1.call-done = bf16[256,128,128]{2,1,0:T(8,128)(2,1)} async-done(((bf16[4,128,128]{2,1,0:T(8,128)(2,1)}), bf16[256,128,128]{2,1,0:T(8,128)(2,1)}) %all-gather.9.cloned.1.call-update) | async-done | bytes 8388624 | tf_op jit(solution)/shard_map/all_gather | solution.py:12
  560.4 142.0 %while.12 = (s32[]{:T(128)}, f32[4,128,128]{2,1,0:T(8,128)S(1)}, s32[]{:T(128)}, bf16[64,4,128,128]{3,2,1,0:T(8,128)(2,1)}, bf16[64,1]{0,1:T(2,128)(2,1)S(1)}, /*index=5*/s32[]{:T(128)}, s32[]{:T(128)}, s32[]{:T(128)}) while((s32[]{:T(128)}, f32[4,128,128]{2,1,0:T(8,128)S(1)}, s32[]{:T(128)}, bf16[64,4,128,128]{3,2,1,0:T(8,128)(2,1)}, ...), condition=%wide.region_2.3_spmd, body=%wide.region_1.2_spmd.sunk | while | flops 196614 | bytes 655505 | solution.py:26
  561.1 1.6 convert_add_fusion.2
  563.3 1.6 convert_add_fusion.2
  565.6 1.6 convert_add_fusion.2
  567.8 1.6 convert_add_fusion.2
  570.1 1.6 convert_add_fusion.2
  572.3 1.6 convert_add_fusion.2
  574.6 1.6 convert_add_fusion.2
  576.8 1.6 convert_add_fusion.2
  579.1 1.6 convert_add_fusion.2
  581.3 1.6 convert_add_fusion.2
  583.6 1.6 convert_add_fusion.2
  585.8 1.6 convert_add_fusion.2
  588.1 1.6 convert_add_fusion.2
  590.3 1.6 convert_add_fusion.2
  592.6 1.6 convert_add_fusion.2
  594.9 1.6 convert_add_fusion.2
  597.1 1.6 convert_add_fusion.2
  599.4 1.6 convert_add_fusion.2
  601.6 1.6 convert_add_fusion.2
  603.9 1.6 convert_add_fusion.2
  606.1 1.6 convert_add_fusion.2
  608.4 1.6 convert_add_fusion.2
  610.6 1.6 convert_add_fusion.2
  612.9 1.6 convert_add_fusion.2
  615.1 1.6 convert_add_fusion.2
  617.4 1.6 convert_add_fusion.2
  619.6 1.6 convert_add_fusion.2
  621.9 1.6 convert_add_fusion.2
  624.1 1.6 convert_add_fusion.2
  626.4 1.6 convert_add_fusion.2
  628.6 1.6 convert_add_fusion.2
  630.9 1.6 convert_add_fusion.2
  633.2 1.6 convert_add_fusion.2
  635.4 1.6 convert_add_fusion.2
  637.7 1.6 convert_add_fusion.2
  639.9 1.6 convert_add_fusion.2
  642.2 1.6 convert_add_fusion.2
  644.4 1.6 convert_add_fusion.2
  646.7 1.6 convert_add_fusion.2
  648.9 1.6 convert_add_fusion.2
  651.2 1.6 convert_add_fusion.2
  653.4 1.6 convert_add_fusion.2
  655.7 1.6 convert_add_fusion.2
  657.9 1.6 convert_add_fusion.2
  660.2 1.6 convert_add_fusion.2
  662.4 1.6 convert_add_fusion.2
  664.7 1.6 convert_add_fusion.2
  667.0 1.6 convert_add_fusion.2
  669.2 1.6 convert_add_fusion.2
  671.5 1.6 convert_add_fusion.2
  673.7 1.6 convert_add_fusion.2
  676.0 1.6 convert_add_fusion.2
  678.2 1.6 convert_add_fusion.2
  680.5 1.6 convert_add_fusion.2
  682.7 1.6 convert_add_fusion.2
  696.2 1.6 convert_add_fusion.2
  698.5 1.6 convert_add_fusion.2
  (100 shorter events, 55.4 us)
Async XLA Ops:
  6.5 199.8 %copy-start = (bf16[1,128,4096]{2,1,0:T(8,128)(2,1)S(1)}, bf16[1,128,4096]{2,1,0:T(8,128)(2,1)}, u32[]{:S(2)}) copy-start(bf16[1,128,4096]{2,1,0:T(8,128)(2,1)} %param.8) | copy-start | bytes 3145732
  6.5 199.8 %all-gather.7.cloned.1.call-start = ((), (), s32[]{:S(2)}) async-start(), calls=%async_computation.1 | async-start | bytes 4202496 | tf_op jit(solution)/shard_map/all_gather | solution.py:45
  7.3 397.1 %all-gather.5.cloned.1.call-start = ((), (), s32[]{:S(2)}) async-start(), calls=%async_computation | async-start | bytes 4202496 | tf_op jit(solution)/shard_map/all_gather | solution.py:44
  8.0 552.4 %all-gather.9.cloned.1.call-start = ((), (), s32[]{:S(2)}) async-start(), calls=%async_computation.2 | async-start | bytes 8519680 | tf_op jit(solution)/shard_map/all_gather | solution.py:12
  209.3 199.7 %copy-start.1 = (bf16[1,128,512]{2,1,0:T(8,128)(2,1)S(1)}, bf16[1,128,512]{2,1,0:T(8,128)(2,1)}, u32[]{:S(2)}) copy-start(bf16[1,128,512]{2,1,0:T(8,128)(2,1)} %param.9) | copy-start | bytes 393220
  407.4 295.7 %copy-start.2 = (f32[512]{0:T(512)S(1)}, f32[512]{0:T(512)}, u32[]{:S(2)}) copy-start(f32[512]{0:T(512)} %param.13) | copy-start | bytes 6148
Sparse Core Ops, SparseCore 0:
  11.9 194.3 all-gather.6
  210.9 193.3 all-gather.4
  408.5 151.8 all-gather.8
where the time goes:
time: 712 us; the launch traced here: 711 us
  waiting for transfers between devices  403 us (57%)
  other arithmetic  142 us (20%)
  blocking collectives  138 us (19%)
  between operations  13.8 us (2%)
  matrix products  7.42 us (1%)
    all_gather x1, waiting for transfers between devices, on_device(): lax.all_gather(w_value, ('ctx', 'fsdp'), axis=0, tiled=True)  196 us
    all_gather x1, waiting for transfers between devices, on_device(): lax.all_gather(w_key, ('ctx', 'fsdp'), axis=0, tiled=True)  195 us
    unnamed x1, blocking collectives  138 us
    add x63, other arithmetic, combine(): return (jnp.maximum(earlier[0], later[0]), later[1] + keep * earlier[1])  104 us
    sub x63, other arithmetic, combine(): keep = 1.0 - later[0][0]  37.1 us
  transfers between devices with their start and end apart: 3, of which 3 were waited for; matrix products, arithmetic and copies ran while one was open for 1% of the time, Pallas kernels for 0%

commit v1 on v0

--- a/solution.py
+++ b/solution.py
@@ -42,7 +42,12 @@
     heads = width // HEAD
     full_panels = (
         lax.all_gather(w_key, ("ctx", "fsdp"), axis=0, tiled=True),
-        lax.all_gather(w_value, ("ctx", "fsdp"), axis=0, tiled=True),
+        jnp.concatenate(
+            lax.all_to_all(
+                jnp.stack([w_value] * lax.axis_size(("ctx", "fsdp"))), ("ctx", "fsdp"), 0, 0
+            ),
+            axis=0,
+        ),
     )
     proj_key = jnp.dot(rows, full_panels[0], preferred_element_type=jnp.float32)
     proj_value = jnp.dot(rows, full_panels[1], preferred_element_type=jnp.float32)

time: 712 us -> 574 us (0.81)
  waiting for transfers between devices: 403 us -> 239 us
  starting transfers between devices: 0.08 us -> 22.6 us
    all_gather x1 -> x0, waiting for transfers between devices: 196 us -> none  [on_device(): lax.all_gather(w_value, ('ctx', 'fsdp'), axis=0, tiled=True)]
    all_gather x1, waiting for transfers between devices: 195 us -> 229 us  [on_device(): lax.all_gather(w_key, ('ctx', 'fsdp'), axis=0, tiled=True)]
    all_to_all x0 -> x1, starting transfers between devices: none -> 22.5 us  [on_device(): lax.all_to_all(jnp.stack([w_value] * lax.axis_size(('ctx', 'fsdp'))), ('c...]
  transfers between devices with their start and end apart: 3 -> 3, of which waited for: 3 -> 2; matrix products, arithmetic and copies ran while one was open for 1% -> 1% of each run, Pallas kernels for 0% -> 0%
where the time goes in v1:
time: 574 us; the launch traced here: 572 us
  waiting for transfers between devices  239 us (42%)
  other arithmetic  142 us (25%)
  blocking collectives  139 us (24%)
  starting transfers between devices  22.6 us (4%)
  between operations  14.2 us (2%)
  matrix products  7.44 us (1%)
  local copies, waits for them, and re-layouts  6.86 us (1%)
    all_gather x1, waiting for transfers between devices, on_device(): lax.all_gather(w_key, ('ctx', 'fsdp'), axis=0, tiled=True)  229 us
    unnamed x1, blocking collectives  139 us
    add x63, other arithmetic, combine(): return (jnp.maximum(earlier[0], later[0]), later[1] + keep * earlier[1])  104 us
    sub x63, other arithmetic, combine(): keep = 1.0 - later[0][0]  37.1 us
    all_to_all x1, starting transfers between devices, on_device(): lax.all_to_all(jnp.stack([w_value] * lax.axis_size(('ctx', 'fsdp'))), ('c...  22.5 us
  transfers between devices with their start and end apart: 3, of which 2 were waited for; matrix products, arithmetic and copies ran while one was open for 1% of the time, Pallas kernels for 0%

profile of v1, /device:TPU:486, one launch (start us, length us, event | category | flops | bytes accessed | tf_op | source)
XLA Modules:
  0.0 572.1 jit_solution(2476046973694068867)
XLA Ops:
  6.5 3.0 stack.2
  9.6 22.5 %all-to-all-start = ((bf16[512,8,512]{2,1,0:T(8,128)(2,1)}), bf16[512,8,512]{2,1,0:T(8,128)(2,1)}, u32[]{:S(2)}, u32[]{:S(2)}) async-start(bf16[512,8,512]{2,1,0:T(8,128)(2,1)} %stack.2), calls=%async_computation | async-start | bytes 8388608 | tf_op jit(solution)/shard_map/all_to_all | solution.py:46
  34.4 228.5 %all-gather.4.cloned.1.call-done = bf16[4096,512]{1,0:T(8,128)(2,1)} async-done(((bf16[8,512]{1,0:T(8,128)(2,1)}), bf16[4096,512]{1,0:T(8,128)(2,1)}) %all-gather.4.cloned.1.call-update) | async-done | bytes 4194320 | tf_op jit(solution)/shard_map/all_gather | solution.py:44
  263.0 3.0 fusion.16
  266.1 2.9 fusion.4
  272.9 138.6 %all-reduce = bf16[64]{0:T(256)(128)(2,1)S(1)} all-reduce(bf16[64]{0:T(256)(128)(2,1)S(1)} %dynamic-update-slice), channel_id=1, replica_groups=mesh['ctx'=64,'fsdp'=8] {'ctx'}, use_global_device_ids=true, to_apply=%add | all-reduce | flops 64 | bytes 256
  411.5 10.2 %all-gather.6.cloned.1.call-done = bf16[256,128,128]{2,1,0:T(8,128)(2,1)} async-done(((bf16[4,128,128]{2,1,0:T(8,128)(2,1)}), bf16[256,128,128]{2,1,0:T(8,128)(2,1)}) %all-gather.6.cloned.1.call-update) | async-done | bytes 8388624 | tf_op jit(solution)/shard_map/all_gather | solution.py:12
  421.7 142.0 %while.12 = (s32[]{:T(128)}, f32[4,128,128]{2,1,0:T(8,128)S(1)}, s32[]{:T(128)}, bf16[64,4,128,128]{3,2,1,0:T(8,128)(2,1)}, bf16[64,1]{0,1:T(2,128)(2,1)S(1)}, /*index=5*/s32[]{:T(128)}, s32[]{:T(128)}, s32[]{:T(128)}) while((s32[]{:T(128)}, f32[4,128,128]{2,1,0:T(8,128)S(1)}, s32[]{:T(128)}, bf16[64,4,128,128]{3,2,1,0:T(8,128)(2,1)}, ...), condition=%wide.region_2.3_spmd, body=%wide.region_1.2_spmd.sunk | while | flops 196614 | bytes 655505 | solution.py:26
  422.3 1.6 convert_add_fusion.2
  424.6 1.6 convert_add_fusion.2
  426.9 1.6 convert_add_fusion.2
  429.1 1.6 convert_add_fusion.2
  431.4 1.6 convert_add_fusion.2
  433.6 1.6 convert_add_fusion.2
  435.9 1.6 convert_add_fusion.2
  438.1 1.6 convert_add_fusion.2
  440.4 1.6 convert_add_fusion.2
  442.6 1.6 convert_add_fusion.2
  444.9 1.6 convert_add_fusion.2
  447.1 1.6 convert_add_fusion.2
  449.4 1.6 convert_add_fusion.2
  451.6 1.6 convert_add_fusion.2
  453.9 1.6 convert_add_fusion.2
  456.1 1.6 convert_add_fusion.2
  458.4 1.6 convert_add_fusion.2
  460.7 1.6 convert_add_fusion.2
  462.9 1.6 convert_add_fusion.2
  465.2 1.6 convert_add_fusion.2
  467.4 1.6 convert_add_fusion.2
  469.7 1.6 convert_add_fusion.2
  471.9 1.6 convert_add_fusion.2
  474.2 1.6 convert_add_fusion.2
  476.4 1.6 convert_add_fusion.2
  478.7 1.6 convert_add_fusion.2
  480.9 1.6 convert_add_fusion.2
  483.2 1.6 convert_add_fusion.2
  485.4 1.6 convert_add_fusion.2
  487.7 1.6 convert_add_fusion.2
  489.9 1.6 convert_add_fusion.2
  492.2 1.6 convert_add_fusion.2
  494.4 1.6 convert_add_fusion.2
  496.7 1.6 convert_add_fusion.2
  499.0 1.6 convert_add_fusion.2
  501.2 1.6 convert_add_fusion.2
  503.5 1.6 convert_add_fusion.2
  505.7 1.6 convert_add_fusion.2
  508.0 1.6 convert_add_fusion.2
  510.2 1.6 convert_add_fusion.2
  512.5 1.6 convert_add_fusion.2
  514.7 1.6 convert_add_fusion.2
  517.0 1.6 convert_add_fusion.2
  519.2 1.6 convert_add_fusion.2
  521.5 1.6 convert_add_fusion.2
  523.7 1.6 convert_add_fusion.2
  526.0 1.6 convert_add_fusion.2
  528.2 1.6 convert_add_fusion.2
  530.5 1.6 convert_add_fusion.2
  532.8 1.6 convert_add_fusion.2
  535.0 1.6 convert_add_fusion.2
  537.3 1.6 convert_add_fusion.2
  539.5 1.6 convert_add_fusion.2
  541.8 1.6 convert_add_fusion.2
  546.3 1.6 convert_add_fusion.2
  548.5 1.6 convert_add_fusion.2
  (102 shorter events, 55.9 us)
Async XLA Ops:
  6.5 256.4 %copy-start = (bf16[1,128,4096]{2,1,0:T(8,128)(2,1)S(1)}, bf16[1,128,4096]{2,1,0:T(8,128)(2,1)}, u32[]{:S(2)}) copy-start(bf16[1,128,4096]{2,1,0:T(8,128)(2,1)} %param.8) | copy-start | bytes 3145732
  9.6 23.3 %copy-start.3 = (s32[1,128]{1,0:T(1,128)S(1)}, s32[1,128]{1,0:T(1,128)}, u32[]{:S(2)}) copy-start(s32[1,128]{1,0:T(1,128)} %param.10) | copy-start | bytes 1540
  9.6 256.6 %all-to-all-start = ((bf16[512,8,512]{2,1,0:T(8,128)(2,1)}), bf16[512,8,512]{2,1,0:T(8,128)(2,1)}, u32[]{:S(2)}, u32[]{:S(2)}) async-start(bf16[512,8,512]{2,1,0:T(8,128)(2,1)} %stack.2), calls=%async_computation | async-start | bytes 8388608 | tf_op jit(solution)/shard_map/all_to_all | solution.py:46
  32.0 230.9 %all-gather.4.cloned.1.call-start = ((), (), s32[]{:S(2)}) async-start(), calls=%async_computation.1 | async-start | bytes 4202496 | tf_op jit(solution)/shard_map/all_gather | solution.py:44
  32.8 388.9 %all-gather.6.cloned.1.call-start = ((), (), s32[]{:S(2)}) async-start(), calls=%async_computation.2 | async-start | bytes 8519680 | tf_op jit(solution)/shard_map/all_gather | solution.py:12
  266.0 4.7 copy-start.1
  269.0 295.3 %copy-start.2 = (f32[512]{0:T(512)S(1)}, f32[512]{0:T(512)}, u32[]{:S(2)}) copy-start(f32[512]{0:T(512)} %param.13) | copy-start | bytes 6148
Sparse Core Ops, SparseCore 0:
  37.5 225.4 all-gather.3
  270.2 151.4 all-gather.5
